TPU v7x, 32 devices: a whole 2x2x4 slice. The times are simulated.
32 devices in a mesh: parts: 2 (over y), dp: 8 (over z, x), grad: 2 (over core).
Axes of the slice: x: 2, y: 2, z: 4, core: 2. Of those that a mesh axis runs over, the one named last changes fastest.
Arguments:
- activations: bfloat16 [32, 14, 14, 1024], P(('parts', 'dp', 'grad')), parts along dimension 0, may hold values from -12 to 12
- output_grads: bfloat16 [32, 14, 14, 1024], P(('parts', 'dp', 'grad')), parts along dimension 0, may hold values from -6 to 6
- owners: int32 [1024, 1], replicated, may hold values from 0 to 7; in each aligned block of 1024 rows (0 to 1023, 1024 to 2047, ...) at most 160 rows name the same one
Outputs:
- owned_inverse: float32 [2560, 2401], P(('parts', 'dp', 'grad')), parts along dimension 0
- update: float32 [49, 2048], P(None, 'parts'), parts along dimension 1
There are 2 independent parts, one for each index of `parts`. A program takes and returns all parts, laid end to end along the dimension named above; an argument that names none is the same for every part. Nothing has to cross between parts.
Inputs may be any that keep to these rules, and one draw needn't show every extreme that they name: `owners`: no owner is named by more than 160 channels; some owner is named by exactly 160.
All inputs are finite; a program needn't handle non-finite values.
Results may differ from a plain program's by a relative error of at most 0.0003.
Values may be sent and summed in bfloat16 or wider, within the bound.
A program may use at most 128 MiB of HBM per device.

v0:
```python
import functools

import jax
import jax.numpy as jnp
from jax import lax
from jax.experimental import pallas as pl
from jax.experimental.pallas import tpu as pltpu
from jax.sharding import PartitionSpec as P

KS = 7
HW = 14
TAPS = 49
PIX = HW * HW
RAD = 3
LANES = 128
PADT = 56
ROWS = 2 * PIX + 8
F32 = jnp.float32
BF16 = jnp.bfloat16
VMEM_LIMIT = 60 * 1024 * 1024


def vmem_specs(count):
    return [pl.BlockSpec(memory_space=pltpu.VMEM)] * count


def route_kernel(slots_dev, capacity, act_ref, grad_ref, ocol_ref, orow_ref, out_ref, srow_ref,
                 data, scol):
    chans = act_ref.shape[1]
    step = pl.program_id(0)

    @pl.when(step == 0)
    def _():
        data[0:PIX, :] = act_ref[...]
        data[PIX:2 * PIX, :] = grad_ref[...]
        data[2 * PIX:ROWS, :] = jnp.ones((8, chans), BF16)
        ocol, orow = ocol_ref[...], orow_ref[...]
        sub = lax.broadcasted_iota(jnp.int32, (chans, chans), 0)
        lane = lax.broadcasted_iota(jnp.int32, (chans, chans), 1)
        same = ocol == orow
        rank_col = jnp.sum(jnp.where(same & (lane < sub), 1.0, 0.0), axis=1, keepdims=True)
        rank_row = jnp.sum(jnp.where(same & (sub < lane), 1.0, 0.0), axis=0, keepdims=True)
        scol[...] = ocol * capacity + rank_col.astype(jnp.int32)
        srow_ref[...] = orow * capacity + rank_row.astype(jnp.int32)

    lane = lax.broadcasted_iota(jnp.int32, (chans, 2 * LANES), 1)
    within = lane & (LANES - 1)
    target = jnp.where(
        within < slots_dev, (2 * step + (lane >> 7)) * slots_dev + within, -1
    )
    pick = jnp.where(scol[...] == target, 1.0, 0.0).astype(BF16)
    got = jnp.dot(data[...], pick, preferred_element_type=F32).astype(BF16)
    out_ref[0] = got[:, :LANES]
    out_ref[1] = got[:, LANES:]


def windows(parts, shift):
    size = abs(shift)
    edge = max(0, RAD - size)
    count = HW - size
    add = lambda items: functools.reduce(lambda p, q: p + q, items)
    mid = add(parts[edge:count - edge])
    if edge == 0:
        return [mid] * (KS - size)
    left, right = parts[:edge], parts[count - edge:]
    grow = [mid + add(left)]
    for item in right:
        grow.append(grow[-1] + item)
    shrink = [mid + add(right)]
    for item in left[:0:-1]:
        shrink.append(shrink[-1] + item)
    full = [grow[-1]] * (KS - size - 2 * edge)
    return grow[:edge] + full + shrink[::-1]


def owner_kernel(imgs, slots_dev, positions, recv_ref, inv_ref, dir_ref,
                 xs, gs, wide, narrow, mat, rowbuf, gbuf, gsum, flat):
    groups = imgs // 8
    scale = 1.0 / positions

    @pl.loop(0, imgs)
    def _(img):
        xs[pl.ds(img, PIX, stride=imgs), :] = recv_ref[img, 0:PIX, :].astype(F32)
        gs[pl.ds(img, PIX, stride=imgs), :] = recv_ref[img, PIX:2 * PIX, :].astype(F32)

    def pixel(ref, row, col, group):
        start = pl.multiple_of((row * HW + col) * imgs + 8 * group, 8)
        return ref[pl.ds(start, 8), :]

    zero = jnp.zeros((8, LANES), F32)

    def total(items):
        return functools.reduce(lambda p, q: p + q, items)

    @pl.loop(0, KS)
    def _(down):
        @pl.loop(0, HW - down)
        def _(row):
            for shift in range(-(KS - 1), KS):
                parts = []
                for col in range(max(0, -shift), HW - max(0, shift)):
                    parts.append(total([
                        pixel(xs, row, col, g) * pixel(xs, row + down, col + shift, g)
                        for g in range(groups)
                    ]))
                sums = windows(parts, shift)
                for place, value in enumerate(sums):
                    b = place + max(0, -shift)
                    start = pl.multiple_of(row * (PADT * 8), 8) + (b * 8 + b + shift) * 8
                    wide[pl.ds(start, 8), :] = value
            for b in range(KS):
                start = pl.multiple_of(row * (PADT * 8), 8) + (b * 8 + 7) * 8
                wide[pl.ds(start, 8), :] = zero

        @pl.loop(0, HW - down)
        def _(row):
            for b in range(KS):
                base = row * (PADT * 8) + b * 64
                value = total([wide[pl.ds(base + s, 8, stride=8), :] for s in range(8)])
                dst = pl.multiple_of((down * HW + row) * PADT, 8) + b * 8
                narrow[pl.ds(dst, 8), :] = value

    sub = lax.broadcasted_iota(jnp.int32, (8, LANES), 0)
    for a in range(KS):
        mat[a * 8 + 7] = jnp.zeros((PADT, LANES), F32)
    for b in range(KS):
        for down in range(KS):
            parts = [
                narrow[(down * HW + row) * PADT + b * 8:(down * HW + row) * PADT + b * 8 + 8, :]
                for row in range(HW - down)
            ]
            for a, value in enumerate(windows(parts, down)):
                value = value * scale
                if down == 0:
                    value = value + jnp.where(sub == b, 0.1, 0.0)
                mat[a * 8 + b, (a + down) * 8:(a + down) * 8 + 8, :] = value
    for a in range(KS):
        for a2 in range(a + 1, KS):
            for b2 in range(KS):
                cols = jnp.concatenate(
                    [mat[a * 8 + b, a2 * 8 + b2:a2 * 8 + b2 + 1, :] for b in range(8)], axis=0
                )
                mat[a2 * 8 + b2, a * 8:a * 8 + 8, :] = cols

    @pl.loop(0, KS)
    def _(a):
        def one(row, sums):
            out = []
            for b in range(KS):
                terms = [sums[b]]
                for col in range(max(0, RAD - b), min(HW, HW + RAD - b)):
                    for g in range(groups):
                        terms.append(
                            pixel(xs, row + a - RAD, col + b - RAD, g) * pixel(gs, row, col, g)
                        )
                out.append(total(terms))
            return tuple(out)

        sums = lax.fori_loop(
            jnp.maximum(0, RAD - a), jnp.minimum(HW, HW + RAD - a), one, (zero,) * KS
        )
        for b in range(KS):
            gbuf[b * 8:b * 8 + 8, :] = sums[b]
        gbuf[56:64, :] = zero
        value = total([gbuf[pl.ds(s, 8, stride=8), :] for s in range(8)])
        gsum[pl.ds(pl.multiple_of(a * 8, 8), 8), :] = value * scale

    def square(row, acc):
        for col in range(HW):
            for g in range(groups):
                value = pixel(gs, row, col, g)
                acc = acc + value * value
        return acc

    stat = jnp.sum(lax.fori_loop(0, HW, square, zero), axis=0, keepdims=True) * scale

    subs = lax.broadcasted_iota(jnp.int32, (PADT, LANES), 0)
    for a in range(KS):
        @pl.loop(0, KS)
        def _(b):
            k = a * 8 + b
            row = mat[k]
            rowbuf[0:PADT, :] = row
            inv = 1.0 / rowbuf[pl.ds(k, 1), :]
            swept = jnp.where(subs == k, -inv, row * inv)
            at_pivot = sub == b
            for i in [p * 8 + q for p in range(KS) for q in range(KS)]:
                coef = jnp.broadcast_to(rowbuf[i:i + 1, :], (8, LANES))
                for tile in range(KS):
                    old = mat[i, tile * 8:tile * 8 + 8, :]
                    if tile == a:
                        old = jnp.where(at_pivot, 0.0, old)
                    mat[i, tile * 8:tile * 8 + 8, :] = old - coef * swept[tile * 8:tile * 8 + 8, :]
            mat[k] = swept

    valid = recv_ref[0, 2 * PIX:ROWS, :].astype(F32)
    acc = jnp.zeros((PADT, LANES), F32)
    for a in range(KS):
        for b in range(KS):
            i = a * 8 + b
            row = mat[i]
            acc = acc - gsum[i:i + 1, :] * row
            for tile in range(KS):
                start = (a * KS + b) * TAPS + tile * KS
                flat[start:start + 8, :] = -row[tile * 8:tile * 8 + 8, :] * valid
    direction = acc / (stat + 0.1)
    product = jnp.sum(direction * gsum[...], axis=0, keepdims=True)
    dir_ref[...] = direction
    dir_ref[7:8, :] = product
    for start in range(0, TAPS * TAPS, LANES):
        width = min(LANES, TAPS * TAPS - start)
        block = jnp.transpose(flat[start:start + LANES, :])
        inv_ref[:, start:start + width] = block[:slots_dev, :width]


def update_kernel(devices_n, slots_dev, chans, dirs_ref, srow_ref, out_ref, acc):
    acc[...] = jnp.zeros_like(acc)
    lane_slot = lax.broadcasted_iota(jnp.int32, (LANES, chans), 0)

    def one(dev, curv):
        value = dirs_ref[dev]
        wanted = srow_ref[...] - dev * slots_dev
        pick = jnp.where((lane_slot == wanted) & (lane_slot < slots_dev), 1.0, 0.0).astype(BF16)
        high = value.astype(BF16)
        rest = value - high.astype(F32)
        mid = rest.astype(BF16)
        low = (rest - mid.astype(F32)).astype(BF16)
        for piece in (high, mid, low):
            acc[...] += jnp.dot(piece, pick, preferred_element_type=F32)
        return curv + value[0:8, :]

    sums = lax.fori_loop(0, devices_n, one, jnp.zeros((8, LANES), F32))
    curvature = jnp.sum(sums[7:8, :], axis=1, keepdims=True)
    factor = jnp.sqrt(TAPS * chans / curvature)
    for a in range(KS):
        out_ref[a * KS:a * KS + KS, :] = acc[a * 8:a * 8 + KS, :] * factor


def route(act, grad, owners, devices_n, slots_dev, capacity):
    chans = act.shape[1]
    whole = lambda *shape: pl.BlockSpec(shape, lambda d: (0,) * len(shape))
    return pl.pallas_call(
        functools.partial(route_kernel, slots_dev, capacity),
        grid=(devices_n // 2,),
        in_specs=[whole(PIX, chans), whole(PIX, chans), whole(chans, 1), whole(1, chans)],
        out_specs=[pl.BlockSpec((2, ROWS, LANES), lambda d: (d, 0, 0)), whole(1, chans)],
        out_shape=[
            jax.ShapeDtypeStruct((devices_n, ROWS, LANES), BF16),
            jax.ShapeDtypeStruct((1, chans), jnp.int32),
        ],
        scratch_shapes=[pltpu.VMEM((ROWS, chans), BF16), pltpu.VMEM((chans, 1), jnp.int32)],
        compiler_params=pltpu.CompilerParams(vmem_limit_bytes=VMEM_LIMIT),
        name="route",
    )(act, grad, owners, owners.reshape(1, chans))


def own(recv, slots_dev, positions):
    imgs = recv.shape[0]
    return pl.pallas_call(
        functools.partial(owner_kernel, imgs, slots_dev, positions),
        in_specs=vmem_specs(1),
        out_specs=vmem_specs(2),
        out_shape=[
            jax.ShapeDtypeStruct((slots_dev, TAPS * TAPS), F32),
            jax.ShapeDtypeStruct((PADT, LANES), F32),
        ],
        scratch_shapes=[
            pltpu.VMEM((PIX * imgs, LANES), F32),
            pltpu.VMEM((PIX * imgs, LANES), F32),
            pltpu.VMEM((HW * PADT * 8, LANES), F32),
            pltpu.VMEM((KS * HW * PADT, LANES), F32),
            pltpu.VMEM((PADT, PADT, LANES), F32),
            pltpu.VMEM((64, LANES), F32),
            pltpu.VMEM((64, LANES), F32),
            pltpu.VMEM((PADT, LANES), F32),
            pltpu.VMEM((19 * LANES, LANES), F32),
        ],
        compiler_params=pltpu.CompilerParams(vmem_limit_bytes=VMEM_LIMIT),
        name="own",
    )(recv)


def spread(dirs, srow, slots_dev):
    devices_n, chans = dirs.shape[0], srow.shape[1]
    return pl.pallas_call(
        functools.partial(update_kernel, devices_n, slots_dev, chans),
        in_specs=vmem_specs(2),
        out_specs=pl.BlockSpec(memory_space=pltpu.VMEM),
        out_shape=jax.ShapeDtypeStruct((TAPS, chans), F32),
        scratch_shapes=[pltpu.VMEM((PADT, chans), F32)],
        compiler_params=pltpu.CompilerParams(vmem_limit_bytes=VMEM_LIMIT),
        name="spread",
    )(dirs, srow)


def per_device(activations, output_grads, owners):
    devices_n = lax.axis_size(("dp", "grad"))
    owners_n = lax.axis_size("dp")
    chans = activations.shape[3]
    capacity = 5 * chans // (4 * owners_n)
    slots_dev = owners_n * capacity // devices_n
    positions = PIX * devices_n
    send, srow = route(
        activations.reshape(PIX, chans), output_grads.reshape(PIX, chans), owners,
        devices_n, slots_dev, capacity,
    )
    recv = lax.all_to_all(send, ("dp", "grad"), 0, 0, tiled=True)
    owned_inverse, direction = own(recv, slots_dev, positions)
    dirs = lax.all_gather(direction, ("dp", "grad"), axis=0, tiled=False)
    return owned_inverse, spread(dirs, srow, slots_dev)


def solution(mesh):
    in_specs = (
        P(("parts", "dp", "grad"), None, None, None),
        P(("parts", "dp", "grad"), None, None, None),
        P(),
    )
    out_specs = (P(("parts", "dp", "grad"), None), P(None, "parts"))
    return jax.shard_map(
        per_device, mesh=mesh, in_specs=in_specs, out_specs=out_specs, check_vma=False
    )
```

profile of v0, /device:TPU:0, one launch (start us, length us, event | category | flops | bytes accessed | tf_op | source)
XLA Modules:
  0.0 114.2 jit_solution(9291540740007770904)
XLA Ops:
  0.6 0.0 copy-start
  0.6 1.9 %reshape.13.act_ref = bf16[196,1024]{1,0:T(8,128)(2,1)} reshape(bf16[1,14,14,1024]{3,2,1,0:T(8,128)(2,1)} %param.3) | data formatting | bytes 802816 | tf_op jit(solution)/shard_map/reshape | solution.py:304
  2.5 1.9 %reshape.14.grad_ref = bf16[196,1024]{1,0:T(8,128)(2,1)} reshape(bf16[1,14,14,1024]{3,2,1,0:T(8,128)(2,1)} %param.4) | data formatting | bytes 802816 | tf_op jit(solution)/shard_map/reshape | solution.py:304
  4.4 0.0 copy-done
  4.4 1.0 copy.5.ocol_ref
  5.5 7.2 %route.1 = (bf16[16,400,128]{2,1,0:T(8,128)(2,1)}, s32[1,1024]{1,0:T(1,128)}) custom-call(bf16[196,1024]{1,0:T(8,128)(2,1)} %reshape.13.act_ref, bf16[196,1024]{1,0:T(8,128)(2,1)} %reshape.14.grad_ref, s32[1024,1]{1,0:T(8,128)} %copy.5.ocol_ref, s32[1,1024]{1,0:T(1,128)} %bitcast.3), custom_call_target="tpu_custom_call" | custom-call | tf_op jit(solution)/shard_map/route/pallas_call | solution.py:242
  12.7 47.2 %all_to_all.5.recv_ref = bf16[16,400,128]{2,1,0:T(8,128)(2,1)} all-to-all(bf16[16,400,128]{2,1,0:T(8,128)(2,1)} %get-tuple-element.6), channel_id=1, replica_groups=mesh['parts'=2,'dp'=8,'grad'=2] {'dp','grad'}, dimensions={0} | all-to-all | bytes 3276800 | tf_op jit(solution)/shard_map/all_to_all | solution.py:307
  59.9 26.8 %own.1 = (f32[80,2401]{1,0:T(8,128)}, f32[56,128]{1,0:T(8,128)}) custom-call(bf16[16,400,128]{2,1,0:T(8,128)(2,1)} %all_to_all.5.recv_ref), custom_call_target="tpu_custom_call" | custom-call | tf_op jit(solution)/shard_map/own/pallas_call | solution.py:259
  86.7 21.6 %all-gather = f32[896,128]{1,0:T(8,128)} all-gather(f32[56,128]{1,0:T(8,128)} %get-tuple-element.8), channel_id=2, replica_groups=mesh['parts'=2,'dp'=8,'grad'=2] {'dp','grad'}, dimensions={0}, use_global_device_ids=true | all-gather | bytes 487424 | tf_op jit(solution)/shard_map/all_gather | solution.py:309
  108.4 5.8 %spread.1 = f32[49,1024]{1,0:T(8,128)} custom-call(f32[16,56,128]{2,1,0:T(8,128)} %bitcast.2, s32[1,1024]{1,0:T(1,128)} %get-tuple-element.9.srow_ref), custom_call_target="tpu_custom_call" | custom-call | tf_op jit(solution)/shard_map/spread/pallas_call | solution.py:285
Async XLA Ops:
  0.6 3.8 %copy-start = (s32[1024,1]{0,1:T(1,128)S(1)}, s32[1024,1]{0,1:T(1,128)}, u32[]{:S(2)}) copy-start(s32[1024,1]{0,1:T(1,128)} %param.5) | copy-start | bytes 12292
where the time goes:
time: 115 us; the launch traced here: 114 us
  blocking collectives  68.9 us (60%)
  Pallas kernels  39.9 us (35%)
  local copies, waits for them, and re-layouts  4.83 us (4%)
    all_to_all x1, blocking collectives, per_device(): recv = lax.all_to_all(send, ('dp', 'grad'), 0, 0, tiled=True)  47.2 us
    pallas_call x1, Pallas kernels, own(): pl.pallas_call(functools.partial(owner_kernel, imgs, slots_dev, positions...  26.8 us
    all_gather x1, blocking collectives, per_device(): dirs = lax.all_gather(direction, ('dp', 'grad'), axis=0, tiled=False)  21.6 us
    pallas_call x1, Pallas kernels, route(): pl.pallas_call(functools.partial(route_kernel, slots_dev, capacity), grid...  7.22 us
    pallas_call x1, Pallas kernels, spread(): pl.pallas_call(functools.partial(update_kernel, devices_n, slots_dev, cha...  5.8 us

commit v1 on v0

--- a/solution.py
+++ b/solution.py
@@ -14,7 +14,9 @@
 RAD = 3
 LANES = 128
 PADT = 56
-ROWS = 2 * PIX + 8
+PIXP = 200
+USED = 80
+MESH = pl.DeviceIdType.MESH
 F32 = jnp.float32
 BF16 = jnp.bfloat16
 VMEM_LIMIT = 60 * 1024 * 1024
@@ -24,34 +26,153 @@
     return [pl.BlockSpec(memory_space=pltpu.VMEM)] * count
 
 
-def route_kernel(slots_dev, capacity, act_ref, grad_ref, ocol_ref, orow_ref, out_ref, srow_ref,
-                 data, scol):
-    chans = act_ref.shape[1]
-    step = pl.program_id(0)
-
-    @pl.when(step == 0)
-    def _():
-        data[0:PIX, :] = act_ref[...]
-        data[PIX:2 * PIX, :] = grad_ref[...]
-        data[2 * PIX:ROWS, :] = jnp.ones((8, chans), BF16)
-        ocol, orow = ocol_ref[...], orow_ref[...]
-        sub = lax.broadcasted_iota(jnp.int32, (chans, chans), 0)
-        lane = lax.broadcasted_iota(jnp.int32, (chans, chans), 1)
-        same = ocol == orow
-        rank_col = jnp.sum(jnp.where(same & (lane < sub), 1.0, 0.0), axis=1, keepdims=True)
-        rank_row = jnp.sum(jnp.where(same & (sub < lane), 1.0, 0.0), axis=0, keepdims=True)
-        scol[...] = ocol * capacity + rank_col.astype(jnp.int32)
-        srow_ref[...] = orow * capacity + rank_row.astype(jnp.int32)
-
-    lane = lax.broadcasted_iota(jnp.int32, (chans, 2 * LANES), 1)
-    within = lane & (LANES - 1)
-    target = jnp.where(
-        within < slots_dev, (2 * step + (lane >> 7)) * slots_dev + within, -1
-    )
-    pick = jnp.where(scol[...] == target, 1.0, 0.0).astype(BF16)
-    got = jnp.dot(data[...], pick, preferred_element_type=F32).astype(BF16)
-    out_ref[0] = got[:, :LANES]
-    out_ref[1] = got[:, LANES:]
+def peer_at(index):
+    cores = lax.axis_size("grad")
+    return {"dp": lax.div(index, cores), "grad": lax.rem(index, cores)}
+
+
+def greet(devices_n, me):
+    barrier = pltpu.get_barrier_semaphore()
+
+    @pl.loop(1, devices_n)
+    def _(off):
+        pl.semaphore_signal(
+            barrier, inc=1, device_id=peer_at(lax.rem(me + off, devices_n)), device_id_type=MESH
+        )
+
+    return barrier
+
+
+def pack(value, lane):
+    one = jnp.where(lane[:72] >= USED, pltpu.roll(value[128:200], 80, 1), value[0:72])
+    two = jnp.where(lane[:56] >= USED, pltpu.roll(value[128:184], 32, 1), value[72:128])
+    far = lane[:16] >= 112
+    return jnp.concatenate([
+        one,
+        jnp.where(far, pltpu.roll(value[184:200], 64, 1), two[0:16]),
+        jnp.where(far, pltpu.roll(value[184:200], 48, 1), two[16:32]),
+        two[32:56],
+    ], axis=0)
+
+
+def unpack(value, lane):
+    head = jnp.where(lane < USED, value, 0.0)
+    low = lane[:72] < 48
+    first = pltpu.roll(value[0:72], 48, 1)
+    rest = jnp.concatenate([
+        pltpu.roll(value[72:128], 96, 1),
+        jnp.where(
+            lane[:16] < 64,
+            pltpu.roll(value[72:88], 64, 1),
+            pltpu.roll(value[88:104], 80, 1),
+        ),
+    ], axis=0)
+    tail = jnp.where(low, first, jnp.where(lane[:72] < USED, rest, 0.0))
+    return head, tail
+
+
+def exchange_kernel(devices_n, owners_n, slots_dev, capacity, act_ref, grad_ref, orow_ref,
+                    recv_ref, srow_ref, stage, data, send, send_sem, recv_sem, self_sem):
+    chans = act_ref.shape[2]
+    me = lax.axis_index(("dp", "grad"))
+    barrier = greet(devices_n, me)
+    for i in range(HW):
+        stage[i * HW:i * HW + HW, :] = act_ref[i].astype(F32)
+        stage[200 + i * HW:200 + i * HW + HW, :] = grad_ref[i].astype(F32)
+    ones = jnp.ones((4, chans), F32)
+    stage[PIX:200, :] = ones
+    stage[200 + PIX:400, :] = ones
+    data[...] = stage[...].astype(BF16)
+    orow = orow_ref[...]
+    mine = lax.broadcasted_iota(jnp.int32, (owners_n, chans), 0) == orow
+    before = jnp.where(
+        lax.broadcasted_iota(jnp.int32, (chans, chans), 0)
+        < lax.broadcasted_iota(jnp.int32, (chans, chans), 1), 1.0, 0.0
+    ).astype(BF16)
+    earlier = jnp.dot(jnp.where(mine, 1.0, 0.0).astype(BF16), before, preferred_element_type=F32)
+    rank = jnp.sum(jnp.where(mine, earlier, 0.0), axis=0, keepdims=True)
+    slot = orow * capacity + rank.astype(jnp.int32)
+    srow_ref[...] = slot
+    lane = lax.broadcasted_iota(jnp.int32, (128, LANES), 1)
+    sub = lax.broadcasted_iota(jnp.int32, (2 * LANES, chans), 0)
+    within = sub & (LANES - 1)
+    offset = jnp.where(within < slots_dev, (sub >> 7) * slots_dev + within, -chans * 8)
+
+    def fill(pair):
+        pick = jnp.where(srow_ref[...] - 2 * pair * slots_dev == offset, 1.0, 0.0).astype(BF16)
+        got = lax.dot_general(
+            data[...], pick, (((1,), (1,)), ((), ())), preferred_element_type=F32
+        )
+        for core in range(2):
+            cols = got[:, core * LANES:(core + 1) * LANES]
+            send[2 * pair + core, 0:128] = pack(cols[0:200], lane).astype(BF16)
+            send[2 * pair + core, 128:256] = pack(cols[200:400], lane).astype(BF16)
+
+    def copy_to(dev):
+        return pltpu.make_async_remote_copy(
+            src_ref=send.at[dev], dst_ref=recv_ref.at[me],
+            send_sem=send_sem.at[dev], recv_sem=recv_sem.at[me],
+            device_id=peer_at(dev), device_id_type=MESH,
+        )
+
+    def copy_from(dev):
+        return pltpu.make_async_remote_copy(
+            src_ref=send.at[dev], dst_ref=recv_ref.at[dev],
+            send_sem=send_sem.at[dev], recv_sem=recv_sem.at[dev],
+            device_id=peer_at(dev), device_id_type=MESH,
+        )
+
+    pairs = devices_n // 2
+    my_pair = lax.div(me, 2)
+    pl.semaphore_wait(barrier, devices_n - 1)
+
+    @pl.loop(1, pairs)
+    def _(off):
+        pair = lax.rem(my_pair + off, pairs)
+        fill(pair)
+        copy_to(2 * pair).start()
+        copy_to(2 * pair + 1).start()
+
+    fill(my_pair)
+    copy_to(4 * my_pair + 1 - me).start()
+    own_copy = pltpu.make_async_copy(send.at[me], recv_ref.at[me], self_sem)
+    own_copy.start()
+
+    @pl.loop(1, devices_n)
+    def _(off):
+        dev = lax.rem(me + off, devices_n)
+        copy_from(dev).wait_send()
+        copy_from(dev).wait_recv()
+
+    own_copy.wait()
+
+
+def gather_kernel(devices_n, dir_ref, out_ref, send_sem, recv_sem, self_sem):
+    me = lax.axis_index(("dp", "grad"))
+    barrier = greet(devices_n, me)
+
+    def copy(dev, block):
+        return pltpu.make_async_remote_copy(
+            src_ref=dir_ref, dst_ref=out_ref.at[block],
+            send_sem=send_sem.at[dev], recv_sem=recv_sem.at[block],
+            device_id=peer_at(dev), device_id_type=MESH,
+        )
+
+    own_copy = pltpu.make_async_copy(dir_ref, out_ref.at[me], self_sem)
+    own_copy.start()
+    pl.semaphore_wait(barrier, devices_n - 1)
+
+    @pl.loop(1, devices_n)
+    def _(off):
+        copy(lax.rem(me + off, devices_n), me).start()
+
+    @pl.loop(1, devices_n)
+    def _(off):
+        dev = lax.rem(me + off, devices_n)
+        copy(dev, dev).wait_send()
+        copy(dev, dev).wait_recv()
+
+    own_copy.wait()
 
 
 def windows(parts, shift):
@@ -78,10 +199,14 @@
     groups = imgs // 8
     scale = 1.0 / positions
 
+    lane = lax.broadcasted_iota(jnp.int32, (128, LANES), 1)
+
     @pl.loop(0, imgs)
     def _(img):
-        xs[pl.ds(img, PIX, stride=imgs), :] = recv_ref[img, 0:PIX, :].astype(F32)
-        gs[pl.ds(img, PIX, stride=imgs), :] = recv_ref[img, PIX:2 * PIX, :].astype(F32)
+        for ref, start in ((xs, 0), (gs, 128)):
+            head, tail = unpack(recv_ref[img, start:start + 128, :].astype(F32), lane)
+            ref[pl.ds(img, 128, stride=imgs), :] = head
+            ref[pl.ds(128 * imgs + img, 72, stride=imgs), :] = tail
 
     def pixel(ref, row, col, group):
         start = pl.multiple_of((row * HW + col) * imgs + 8 * group, 8)
@@ -193,7 +318,7 @@
                     mat[i, tile * 8:tile * 8 + 8, :] = old - coef * swept[tile * 8:tile * 8 + 8, :]
             mat[k] = swept
 
-    valid = recv_ref[0, 2 * PIX:ROWS, :].astype(F32)
+    valid = jnp.broadcast_to(xs[PIX * imgs:PIX * imgs + 1, :], (8, LANES))
     acc = jnp.zeros((PADT, LANES), F32)
     for a in range(KS):
         for b in range(KS):
@@ -236,22 +361,45 @@
         out_ref[a * KS:a * KS + KS, :] = acc[a * 8:a * 8 + KS, :] * factor
 
 
-def route(act, grad, owners, devices_n, slots_dev, capacity):
-    chans = act.shape[1]
-    whole = lambda *shape: pl.BlockSpec(shape, lambda d: (0,) * len(shape))
+def exchange(act, grad, owners, devices_n, owners_n, slots_dev, capacity):
+    chans = act.shape[2]
     return pl.pallas_call(
-        functools.partial(route_kernel, slots_dev, capacity),
-        grid=(devices_n // 2,),
-        in_specs=[whole(PIX, chans), whole(PIX, chans), whole(chans, 1), whole(1, chans)],
-        out_specs=[pl.BlockSpec((2, ROWS, LANES), lambda d: (d, 0, 0)), whole(1, chans)],
+        functools.partial(exchange_kernel, devices_n, owners_n, slots_dev, capacity),
+        in_specs=vmem_specs(3),
+        out_specs=[pl.BlockSpec(memory_space=pl.ANY), pl.BlockSpec(memory_space=pltpu.VMEM)],
         out_shape=[
-            jax.ShapeDtypeStruct((devices_n, ROWS, LANES), BF16),
+            jax.ShapeDtypeStruct((devices_n, 256, LANES), BF16),
             jax.ShapeDtypeStruct((1, chans), jnp.int32),
         ],
-        scratch_shapes=[pltpu.VMEM((ROWS, chans), BF16), pltpu.VMEM((chans, 1), jnp.int32)],
-        compiler_params=pltpu.CompilerParams(vmem_limit_bytes=VMEM_LIMIT),
-        name="route",
-    )(act, grad, owners, owners.reshape(1, chans))
+        scratch_shapes=[
+            pltpu.VMEM((2 * PIXP, chans), F32),
+            pltpu.VMEM((2 * PIXP, chans), BF16),
+            pltpu.VMEM((devices_n, 256, LANES), BF16),
+            pltpu.SemaphoreType.DMA((devices_n,)),
+            pltpu.SemaphoreType.DMA((devices_n,)),
+            pltpu.SemaphoreType.DMA,
+        ],
+        compiler_params=pltpu.CompilerParams(
+            collective_id=0, has_side_effects=True, vmem_limit_bytes=VMEM_LIMIT
+        ),
+        name="exchange",
+    )(act, grad, owners.reshape(1, chans))
+
+
+def gather(direction, devices_n):
+    return pl.pallas_call(
+        functools.partial(gather_kernel, devices_n),
+        in_specs=vmem_specs(1),
+        out_specs=pl.BlockSpec(memory_space=pltpu.VMEM),
+        out_shape=jax.ShapeDtypeStruct((devices_n,) + direction.shape, F32),
+        scratch_shapes=[
+            pltpu.SemaphoreType.DMA((devices_n,)),
+            pltpu.SemaphoreType.DMA((devices_n,)),
+            pltpu.SemaphoreType.DMA,
+        ],
+        compiler_params=pltpu.CompilerParams(collective_id=1, has_side_effects=True),
+        name="gather",
+    )(direction)
 
 
 def own(recv, slots_dev, positions):
@@ -265,8 +413,8 @@
             jax.ShapeDtypeStruct((PADT, LANES), F32),
         ],
         scratch_shapes=[
-            pltpu.VMEM((PIX * imgs, LANES), F32),
-            pltpu.VMEM((PIX * imgs, LANES), F32),
+            pltpu.VMEM((PIXP * imgs, LANES), F32),
+            pltpu.VMEM((PIXP * imgs, LANES), F32),
             pltpu.VMEM((HW * PADT * 8, LANES), F32),
             pltpu.VMEM((KS * HW * PADT, LANES), F32),
             pltpu.VMEM((PADT, PADT, LANES), F32),
@@ -300,13 +448,11 @@
     capacity = 5 * chans // (4 * owners_n)
     slots_dev = owners_n * capacity // devices_n
     positions = PIX * devices_n
-    send, srow = route(
-        activations.reshape(PIX, chans), output_grads.reshape(PIX, chans), owners,
-        devices_n, slots_dev, capacity,
+    recv, srow = exchange(
+        activations[0], output_grads[0], owners, devices_n, owners_n, slots_dev, capacity
     )
-    recv = lax.all_to_all(send, ("dp", "grad"), 0, 0, tiled=True)
     owned_inverse, direction = own(recv, slots_dev, positions)
-    dirs = lax.all_gather(direction, ("dp", "grad"), axis=0, tiled=False)
+    dirs = gather(direction, devices_n)
     return owned_inverse, spread(dirs, srow, slots_dev)
 
 

time: 115 us -> 80.4 us (0.70)
  blocking collectives: 68.9 us -> 0 us
  Pallas kernels: 39.9 us -> 78.4 us
  local copies, waits for them, and re-layouts: 4.83 us -> 0 us
    all_to_all x1 -> x0, blocking collectives: 47.2 us -> none  [per_device(): recv = lax.all_to_all(send, ('dp', 'grad'), 0, 0, tiled=True)]
    pallas_call x1 -> x2, Pallas kernels: 7.22 us -> 45.7 us  [the longest x1 26.5 us: exchange(): pl.pallas_call(functools.partial(exchange_kernel, devices_n, owners_n, sl...]
    all_gather x1 -> x0, blocking collectives: 21.6 us -> none  [per_device(): dirs = lax.all_gather(direction, ('dp', 'grad'), axis=0, tiled=False)]
    reshape x2 -> x0, local copies, waits for them, and re-layouts: 3.8 us -> none  [the longest x1 1.9 us: per_device(): activations.reshape(PIX, chans)]
where the time goes in v1:
time: 80.4 us; the launch traced here: 79.1 us
  Pallas kernels  78.4 us (98%)
    pallas_call x1, Pallas kernels, own(): pl.pallas_call(functools.partial(owner_kernel, imgs, slots_dev, positions...  26.9 us
    pallas_call x1, Pallas kernels, exchange(): pl.pallas_call(functools.partial(exchange_kernel, devices_n, owners_n, sl...  26.5 us
    pallas_call x1, Pallas kernels, gather(): pl.pallas_call(functools.partial(gather_kernel, devices_n), in_specs=vmem...  19.2 us
    pallas_call x1, Pallas kernels, spread(): pl.pallas_call(functools.partial(update_kernel, devices_n, slots_dev, cha...  5.81 us

profile of v1, /device:TPU:0, one launch (start us, length us, event | category | flops | bytes accessed | tf_op | source)
XLA Modules:
  0.0 79.1 jit_solution(1415942848462821850)
XLA Ops:
  0.6 26.5 %exchange.1 = (bf16[16,256,128]{2,1,0:T(8,128)(2,1)}, s32[1,1024]{1,0:T(1,128)}) custom-call(bf16[14,14,1024]{2,1,0:T(8,128)(2,1)} %bitcast.3, bf16[14,14,1024]{2,1,0:T(8,128)(2,1)} %bitcast.4, s32[1,1024]{1,0:T(1,128)} %bitcast.5), custom_call_target="tpu_custom_call" | custom-call | tf_op jit(solution)/shard_map/exchange/pallas_call | solution.py:366
  27.1 26.9 %own.1 = (f32[80,2401]{1,0:T(8,128)}, f32[56,128]{1,0:T(8,128)}) custom-call(bf16[16,256,128]{2,1,0:T(8,128)(2,1)} %get-tuple-element.6.recv_ref), custom_call_target="tpu_custom_call" | custom-call | tf_op jit(solution)/shard_map/own/pallas_call | solution.py:407
  54.0 19.2 %gather.1.dirs_ref = f32[16,56,128]{2,1,0:T(8,128)} custom-call(f32[56,128]{1,0:T(8,128)} %get-tuple-element.8.dir_ref), custom_call_target="tpu_custom_call" | custom-call | tf_op jit(solution)/shard_map/gather/pallas_call | solution.py:390
  73.3 5.8 %spread.1 = f32[49,1024]{1,0:T(8,128)} custom-call(f32[16,56,128]{2,1,0:T(8,128)} %gather.1.dirs_ref, s32[1,1024]{1,0:T(1,128)} %get-tuple-element.9.srow_ref), custom_call_target="tpu_custom_call" | custom-call | tf_op jit(solution)/shard_map/spread/pallas_call | solution.py:433

commit v2 on v1

--- a/solution.py
+++ b/solution.py
@@ -126,8 +126,10 @@
     my_pair = lax.div(me, 2)
     pl.semaphore_wait(barrier, devices_n - 1)
 
-    @pl.loop(1, pairs)
-    def _(off):
+    @pl.loop(0, pairs - 1)
+    def _(turn):
+        side = 2 * lax.rem(turn, 2) - 1
+        off = pairs // 2 + side * lax.div(turn + 1, 2)
         pair = lax.rem(my_pair + off, pairs)
         fill(pair)
         copy_to(2 * pair).start()
@@ -147,32 +149,89 @@
     own_copy.wait()
 
 
-def gather_kernel(devices_n, dir_ref, out_ref, send_sem, recv_sem, self_sem):
+def gather_kernel(devices_n, slots_dev, chans, dir_ref, srow_ref, out_ref,
+                  dirs, acc, send_sem, recv_sem, pass_sem):
     me = lax.axis_index(("dp", "grad"))
+    pairs = devices_n // 2
+    my_pair = lax.div(me, 2)
+    core = me - 2 * my_pair
+    sibling = 2 * my_pair + 1 - core
     barrier = greet(devices_n, me)
 
-    def copy(dev, block):
+    def near(off):
+        return 2 * lax.rem(my_pair + off, pairs) + core
+
+    def far(off):
+        return 2 * lax.rem(my_pair + off, pairs) + 1 - core
+
+    def direct(dev, block):
         return pltpu.make_async_remote_copy(
-            src_ref=dir_ref, dst_ref=out_ref.at[block],
+            src_ref=dir_ref, dst_ref=dirs.at[block],
             send_sem=send_sem.at[dev], recv_sem=recv_sem.at[block],
             device_id=peer_at(dev), device_id_type=MESH,
         )
 
-    own_copy = pltpu.make_async_copy(dir_ref, out_ref.at[me], self_sem)
-    own_copy.start()
+    def passed(block, landing):
+        return pltpu.make_async_remote_copy(
+            src_ref=dirs.at[block], dst_ref=dirs.at[landing],
+            send_sem=pass_sem.at[block], recv_sem=recv_sem.at[landing],
+            device_id=peer_at(sibling), device_id_type=MESH,
+        )
+
+    lane_slot = lax.broadcasted_iota(jnp.int32, (LANES, chans), 0)
+    lane_slot = jnp.where(lane_slot < slots_dev, lane_slot, -8 * chans)
+
+    def place(dev, value):
+        pick = jnp.where(lane_slot == srow_ref[...] - dev * slots_dev, 1.0, 0.0).astype(BF16)
+        high = value.astype(BF16)
+        rest = value - high.astype(F32)
+        mid = rest.astype(BF16)
+        low = (rest - mid.astype(F32)).astype(BF16)
+        return (
+            jnp.dot(high, pick, preferred_element_type=F32)
+            + jnp.dot(mid, pick, preferred_element_type=F32)
+            + jnp.dot(low, pick, preferred_element_type=F32)
+        )
+
     pl.semaphore_wait(barrier, devices_n - 1)
 
-    @pl.loop(1, devices_n)
+    @pl.loop(1, pairs)
     def _(off):
-        copy(lax.rem(me + off, devices_n), me).start()
-
-    @pl.loop(1, devices_n)
+        direct(near(off), me).start()
+
+    direct(sibling, me).start()
+    acc[...] = place(me, dir_ref[...])
+
+    def take_near(off, curv):
+        dev = near(off)
+        direct(dev, dev).wait_recv()
+        passed(dev, dev).start()
+        value = dirs[dev]
+        acc[...] += place(dev, value)
+        return curv + value[0:8, :]
+
+    curv = lax.fori_loop(1, pairs, take_near, dir_ref[0:8, :])
+
+    def take_far(off, curv):
+        dev = far(off)
+        passed(dev, dev).wait_recv()
+        value = dirs[dev]
+        acc[...] += place(dev, value)
+        return curv + value[0:8, :]
+
+    curv = lax.fori_loop(0, pairs, take_far, curv)
+
+    @pl.loop(1, pairs)
     def _(off):
-        dev = lax.rem(me + off, devices_n)
-        copy(dev, dev).wait_send()
-        copy(dev, dev).wait_recv()
-
-    own_copy.wait()
+        dev = near(off)
+        direct(dev, dev).wait_send()
+        passed(dev, dev).wait_send()
+
+    direct(sibling, sibling).wait_send()
+    curvature = jnp.sum(curv[7:8, :], axis=1, keepdims=True)
+    factor = jnp.sqrt(TAPS * chans / curvature)
+    for a in range(KS):
+        out_ref[a * KS:a * KS + KS, :] = acc[a * 8:a * 8 + KS, :] * factor
 
 
 def windows(parts, shift):
@@ -336,29 +395,6 @@
         width = min(LANES, TAPS * TAPS - start)
         block = jnp.transpose(flat[start:start + LANES, :])
         inv_ref[:, start:start + width] = block[:slots_dev, :width]
-
-
-def update_kernel(devices_n, slots_dev, chans, dirs_ref, srow_ref, out_ref, acc):
-    acc[...] = jnp.zeros_like(acc)
-    lane_slot = lax.broadcasted_iota(jnp.int32, (LANES, chans), 0)
-
-    def one(dev, curv):
-        value = dirs_ref[dev]
-        wanted = srow_ref[...] - dev * slots_dev
-        pick = jnp.where((lane_slot == wanted) & (lane_slot < slots_dev), 1.0, 0.0).astype(BF16)
-        high = value.astype(BF16)
-        rest = value - high.astype(F32)
-        mid = rest.astype(BF16)
-        low = (rest - mid.astype(F32)).astype(BF16)
-        for piece in (high, mid, low):
-            acc[...] += jnp.dot(piece, pick, preferred_element_type=F32)
-        return curv + value[0:8, :]
-
-    sums = lax.fori_loop(0, devices_n, one, jnp.zeros((8, LANES), F32))
-    curvature = jnp.sum(sums[7:8, :], axis=1, keepdims=True)
-    factor = jnp.sqrt(TAPS * chans / curvature)
-    for a in range(KS):
-        out_ref[a * KS:a * KS + KS, :] = acc[a * 8:a * 8 + KS, :] * factor
 
 
 def exchange(act, grad, owners, devices_n, owners_n, slots_dev, capacity):
@@ -386,20 +422,25 @@
     )(act, grad, owners.reshape(1, chans))
 
 
-def gather(direction, devices_n):
+def gather(direction, srow, devices_n, slots_dev):
+    chans = srow.shape[1]
     return pl.pallas_call(
-        functools.partial(gather_kernel, devices_n),
-        in_specs=vmem_specs(1),
+        functools.partial(gather_kernel, devices_n, slots_dev, chans),
+        in_specs=vmem_specs(2),
         out_specs=pl.BlockSpec(memory_space=pltpu.VMEM),
-        out_shape=jax.ShapeDtypeStruct((devices_n,) + direction.shape, F32),
+        out_shape=jax.ShapeDtypeStruct((TAPS, chans), F32),
         scratch_shapes=[
+            pltpu.VMEM((devices_n, PADT, LANES), F32),
+            pltpu.VMEM((PADT, chans), F32),
             pltpu.SemaphoreType.DMA((devices_n,)),
             pltpu.SemaphoreType.DMA((devices_n,)),
-            pltpu.SemaphoreType.DMA,
+            pltpu.SemaphoreType.DMA((devices_n,)),
         ],
-        compiler_params=pltpu.CompilerParams(collective_id=1, has_side_effects=True),
+        compiler_params=pltpu.CompilerParams(
+            collective_id=1, has_side_effects=True, vmem_limit_bytes=VMEM_LIMIT
+        ),
         name="gather",
-    )(direction)
+    )(direction, srow)
 
 
 def own(recv, slots_dev, positions):
@@ -428,19 +469,6 @@
     )(recv)
 
 
-def spread(dirs, srow, slots_dev):
-    devices_n, chans = dirs.shape[0], srow.shape[1]
-    return pl.pallas_call(
-        functools.partial(update_kernel, devices_n, slots_dev, chans),
-        in_specs=vmem_specs(2),
-        out_specs=pl.BlockSpec(memory_space=pltpu.VMEM),
-        out_shape=jax.ShapeDtypeStruct((TAPS, chans), F32),
-        scratch_shapes=[pltpu.VMEM((PADT, chans), F32)],
-        compiler_params=pltpu.CompilerParams(vmem_limit_bytes=VMEM_LIMIT),
-        name="spread",
-    )(dirs, srow)
-
-
 def per_device(activations, output_grads, owners):
     devices_n = lax.axis_size(("dp", "grad"))
     owners_n = lax.axis_size("dp")
@@ -452,8 +480,7 @@
         activations[0], output_grads[0], owners, devices_n, owners_n, slots_dev, capacity
     )
     owned_inverse, direction = own(recv, slots_dev, positions)
-    dirs = gather(direction, devices_n)
-    return owned_inverse, spread(dirs, srow, slots_dev)
+    return owned_inverse, gather(direction, srow, devices_n, slots_dev)
 
 
 def solution(mesh):

time: 80.4 us -> 74.3 us (0.924); the launches traced: 79.1 us -> 74 us
  Pallas kernels: 78.4 us -> 71.7 us
  local copies, waits for them, and re-layouts: 0 us -> 1.64 us
    pallas_call x2 -> x1, Pallas kernels: 25 us -> 16.2 us  [gather(): pl.pallas_call(functools.partial(gather_kernel, devices_n, slots_dev, cha...]
    pallas_call x1, Pallas kernels: 26.5 us -> 28.5 us  [exchange(): pl.pallas_call(functools.partial(exchange_kernel, devices_n, owners_n, sl...]
    unnamed x0 -> x1, local copies, waits for them, and re-layouts: none -> 1.64 us
where the time goes in v2:
time: 74.3 us; the launch traced here: 74 us
  Pallas kernels  71.7 us (97%)
  local copies, waits for them, and re-layouts  1.64 us (2%)
    pallas_call x1, Pallas kernels, exchange(): pl.pallas_call(functools.partial(exchange_kernel, devices_n, owners_n, sl...  28.5 us
    pallas_call x1, Pallas kernels, own(): pl.pallas_call(functools.partial(owner_kernel, imgs, slots_dev, positions...  26.9 us
    pallas_call x1, Pallas kernels, gather(): pl.pallas_call(functools.partial(gather_kernel, devices_n, slots_dev, cha...  16.2 us
    unnamed x1, local copies, waits for them, and re-layouts  1.64 us

profile of v2, /device:TPU:0, one launch (start us, length us, event | category | flops | bytes accessed | tf_op | source)
XLA Modules:
  0.0 74.0 jit_solution(16117506386866803014)
XLA Ops:
  0.6 28.5 %exchange.1 = (bf16[16,256,128]{2,1,0:T(8,128)(2,1)}, s32[1,1024]{1,0:T(1,128)}) custom-call(bf16[14,14,1024]{2,1,0:T(8,128)(2,1)} %bitcast.3, bf16[14,14,1024]{2,1,0:T(8,128)(2,1)} %bitcast.4, s32[1,1024]{1,0:T(1,128)} %bitcast.5), custom_call_target="tpu_custom_call" | custom-call | tf_op jit(solution)/shard_map/exchange/pallas_call | solution.py:402
  29.2 26.9 %own.1 = (f32[80,2401]{1,0:T(8,128)}, f32[56,128]{1,0:T(8,128)}) custom-call(bf16[16,256,128]{2,1,0:T(8,128)(2,1)} %get-tuple-element.6.recv_ref), custom_call_target="tpu_custom_call" | custom-call | tf_op jit(solution)/shard_map/own/pallas_call | solution.py:448
  56.1 16.2 %gather.1 = f32[49,1024]{1,0:T(8,128)} custom-call(f32[56,128]{1,0:T(8,128)} %get-tuple-element.8.dir_ref, s32[1,1024]{1,0:T(1,128)} %get-tuple-element.9.srow_ref), custom_call_target="tpu_custom_call" | custom-call | tf_op jit(solution)/shard_map/gather/pallas_call | solution.py:427
  72.3 1.6 %copy.6 = f32[49,1024]{1,0:T(8,128)} copy(f32[49,1024]{1,0:T(8,128)} %gather.1) | data formatting | bytes 401408

commit v3 on v2

--- a/solution.py
+++ b/solution.py
@@ -280,11 +280,12 @@
     def _(down):
         @pl.loop(0, HW - down)
         def _(row):
+            here = [[pixel(xs, row, col, g) for g in range(groups)] for col in range(HW)]
             for shift in range(-(KS - 1), KS):
                 parts = []
                 for col in range(max(0, -shift), HW - max(0, shift)):
                     parts.append(total([
-                        pixel(xs, row, col, g) * pixel(xs, row + down, col + shift, g)
+                        here[col][g] * pixel(xs, row + down, col + shift, g)
                         for g in range(groups)
                     ]))
                 sums = windows(parts, shift)
@@ -330,12 +331,13 @@
     def _(a):
         def one(row, sums):
             out = []
+            here = [[pixel(gs, row, col, g) for g in range(groups)] for col in range(HW)]
             for b in range(KS):
                 terms = [sums[b]]
                 for col in range(max(0, RAD - b), min(HW, HW + RAD - b)):
                     for g in range(groups):
                         terms.append(
-                            pixel(xs, row + a - RAD, col + b - RAD, g) * pixel(gs, row, col, g)
+                            pixel(xs, row + a - RAD, col + b - RAD, g) * here[col][g]
                         )
                 out.append(total(terms))
             return tuple(out)

time: 74.3 us -> 74.6 us (level)
  no operation moved by 1% of the time
where the time goes in v3:
time: 74.6 us; the launch traced here: 74.2 us
  Pallas kernels  71.9 us (96%)
  local copies, waits for them, and re-layouts  1.64 us (2%)
    pallas_call x1, Pallas kernels, exchange(): pl.pallas_call(functools.partial(exchange_kernel, devices_n, owners_n, sl...  28.5 us
    pallas_call x1, Pallas kernels, own(): pl.pallas_call(functools.partial(owner_kernel, imgs, slots_dev, positions...  27.1 us
    pallas_call x1, Pallas kernels, gather(): pl.pallas_call(functools.partial(gather_kernel, devices_n, slots_dev, cha...  16.2 us
    unnamed x1, local copies, waits for them, and re-layouts  1.64 us

profile of v3, /device:TPU:0, one launch (start us, length us, event | category | flops | bytes accessed | tf_op | source)
XLA Modules:
  0.0 74.2 jit_solution(8105865352890581799)
XLA Ops:
  0.6 28.5 %exchange.1 = (bf16[16,256,128]{2,1,0:T(8,128)(2,1)}, s32[1,1024]{1,0:T(1,128)}) custom-call(bf16[14,14,1024]{2,1,0:T(8,128)(2,1)} %bitcast.3, bf16[14,14,1024]{2,1,0:T(8,128)(2,1)} %bitcast.4, s32[1,1024]{1,0:T(1,128)} %bitcast.5), custom_call_target="tpu_custom_call" | custom-call | tf_op jit(solution)/shard_map/exchange/pallas_call | solution.py:404
  29.2 27.1 %own.1 = (f32[80,2401]{1,0:T(8,128)}, f32[56,128]{1,0:T(8,128)}) custom-call(bf16[16,256,128]{2,1,0:T(8,128)(2,1)} %get-tuple-element.6.recv_ref), custom_call_target="tpu_custom_call" | custom-call | tf_op jit(solution)/shard_map/own/pallas_call | solution.py:450
  56.3 16.2 %gather.1 = f32[49,1024]{1,0:T(8,128)} custom-call(f32[56,128]{1,0:T(8,128)} %get-tuple-element.8.dir_ref, s32[1,1024]{1,0:T(1,128)} %get-tuple-element.9.srow_ref), custom_call_target="tpu_custom_call" | custom-call | tf_op jit(solution)/shard_map/gather/pallas_call | solution.py:429
  72.6 1.6 %copy.6 = f32[49,1024]{1,0:T(8,128)} copy(f32[49,1024]{1,0:T(8,128)} %gather.1) | data formatting | bytes 401408
